TPU v7x, 32 devices: a whole 2x2x4 slice. The times are simulated.
32 devices in a mesh: dp: 8 (over y, x, core), mp: 4 (over z).
Axes of the slice: x: 2, y: 2, z: 4, core: 2. Of those that a mesh axis runs over, the one named last changes fastest.
Arguments:
- token_ids: int32 [8, 1024], P('dp'), may hold values from 0 to 50303
- prompt_len: int32 [8], replicated, may hold values from 1 to 512, as said below
- example_len: int32 [8], replicated, may hold values from 512 to 1024, as said below
- embedding: bfloat16 [50304, 1024], P('mp'), may hold values from -6 to 6
- w_qkv: bfloat16 [1024, 3072], P(None, 'mp'), may hold values from -0.1875 to 0.1875
- w_out: bfloat16 [1024, 1024], P('mp'), may hold values from -0.75 to 0.75
- w_in: bfloat16 [1024, 4096], P(None, 'mp'), may hold values from -0.1875 to 0.1875
- b_in: float32 [4096], P('mp'), may hold values from -3 to 3
- w_down: bfloat16 [4096, 1024], P('mp'), may hold values from -0.09375 to 0.09375
- unembed: bfloat16 [1024, 50304], P('dp', 'mp'), may hold values from -0.1875 to 0.1875
- ln_gain: float32 [3, 1024], replicated, may hold values from 0.5 to 1.5
- ln_bias: float32 [3, 1024], replicated, may hold values from -3 to 3
- master: float32 [8, 1024, 128], P(None, ('dp', 'mp')), may hold values from -0.1875 to 0.1875
- first_moment: float32 [8, 1024, 128], P(None, ('dp', 'mp')), may hold values from -1.5258789e-05 to 1.5258789e-05
- second_moment: float32 [8, 1024, 128], P(None, ('dp', 'mp')), may hold values from 4.7683716e-14 to 7.6293946e-13
- eigen_bases: float32 [8, 128, 128], replicated, as said below
Outputs:
- mean_loss: float32 [], replicated
- grad_norm: float32 [], replicated
- new_first: float32 [8, 1024, 128], P(None, ('dp', 'mp'))
- new_second: float32 [8, 1024, 128], P(None, ('dp', 'mp'))
- new_master: float32 [8, 1024, 128], P(None, ('dp', 'mp'))
Inputs may be any that keep to these rules, and one draw needn't show every extreme that they name: `prompt_len`: each at most half of its example's length; the first example's is 512. `example_len`: the first example is 1024 tokens long. `eigen_bases`: each matrix is orthogonal.
All inputs are finite; a program needn't handle non-finite values.
Results may differ from a plain program's by a relative error of at most 0.0024.
Values may be sent and summed in bfloat16 or wider, within the bound.
A program may use at most 192 MiB of HBM per device.

v0:
```python
import jax
import jax.numpy as jnp
from jax import lax
from jax.sharding import PartitionSpec as P

D = 1024
HEADS = 16
R = 128
ADAM_STEP = 10
HD = 64
ROT = 16
HIGH_PRECISION = lax.Precision.HIGHEST
NORM_EPS = 1e-05
ROPE_BASE = 10000.0
CLIP_LIMIT = 0.01
LEARN_RATE = 0.02
BETA_FIRST = 0.9
BETA_SECOND = 0.999
ADAM_EPS = 1e-08
DECAY_RATE = 0.01


def merged(value, axis, join):
    pieces = jax.tree.map(lambda part: lax.all_gather(part, axis), value)
    head = jax.tree.map(lambda part: part[0], pieces)
    tail = jax.tree.map(lambda part: part[1:], pieces)
    running, _ = lax.scan(lambda running, section: (join(running, section), None), head, tail)
    return running


def layer_norm(values, gain, shift):
    centre = values - jnp.mean(values, -1, keepdims=True)
    spread = jnp.mean(centre * centre, -1, keepdims=True)
    return centre * lax.rsqrt(spread + NORM_EPS) * gain + shift


def norm_back(values, gain, shift, upstream):
    _, pullback = jax.vjp(lambda inputs: layer_norm(inputs, gain, shift), values)
    return pullback(upstream)[0]


def rope_tables(length):
    half = ROT // 2
    freqs = ROPE_BASE ** (-2.0 * jnp.arange(half, dtype=jnp.float32) / ROT)
    angles = jnp.arange(length, dtype=jnp.float32)[:, None] * freqs[None, :]
    return (jnp.cos(angles)[:, None, :], jnp.sin(angles)[:, None, :])


def rotate(field, cosine, sine):
    half = ROT // 2
    first = field[..., :half]
    second = field[..., half:ROT]
    return jnp.concatenate(
        [first * cosine - second * sine, second * cosine + first * sine, field[..., ROT:]], -1
    )


def rotate_back(upstream, cosine, sine):
    half = ROT // 2
    first = upstream[..., :half]
    second = upstream[..., half:ROT]
    return jnp.concatenate(
        [first * cosine + second * sine, second * cosine - first * sine, upstream[..., ROT:]], -1
    )


def masked_scores(queries, key_rows, start_row, stop_row):
    scores = jnp.einsum(
        "qhd,khd->hqk",
        queries[start_row:stop_row],
        key_rows[:stop_row],
        preferred_element_type=jnp.float32,
    ) * HD ** (-0.5)
    query_pos = start_row + jnp.arange(stop_row - start_row)[:, None]
    causal = jnp.arange(stop_row)[None, :] <= query_pos
    return jnp.where(causal[None], scores, -1e30)


def attend(queries, key_rows, value_rows):
    length = queries.shape[0]
    row_block = min(512, length)
    outputs = []
    spreads = []
    for start_row in range(0, length, row_block):
        stop_row = start_row + row_block
        scores = masked_scores(queries, key_rows, start_row, stop_row)
        top_score = jnp.max(scores, -1, keepdims=True)
        weights = jnp.exp(scores - top_score)
        row_total = jnp.sum(weights, -1, keepdims=True)
        probs = (weights / row_total).astype(jnp.bfloat16)
        outputs.append(
            jnp.einsum(
                "hqk,khd->qhd", probs, value_rows[:stop_row], preferred_element_type=jnp.float32
            )
        )
        spreads.append((top_score + jnp.log(row_total))[..., 0])
    return (jnp.concatenate(outputs, 0).astype(jnp.bfloat16), jnp.concatenate(spreads, 1))


def attend_back(queries, key_rows, value_rows, spreads, upstream):
    length = queries.shape[0]
    row_block = min(512, length)
    scaling = HD ** (-0.5)
    query_grads = []
    key_grad = jnp.zeros(key_rows.shape, jnp.float32)
    value_grad = jnp.zeros(value_rows.shape, jnp.float32)
    for start_row in range(0, length, row_block):
        stop_row = start_row + row_block
        scores = masked_scores(queries, key_rows, start_row, stop_row)
        probs = jnp.exp(scores - spreads[:, start_row:stop_row, None])
        grad_here = upstream[start_row:stop_row]
        prob_grad = jnp.einsum(
            "qhd,khd->hqk", grad_here, value_rows[:stop_row], preferred_element_type=jnp.float32
        )
        inner_sum = jnp.sum(probs * prob_grad, -1, keepdims=True)
        score_grad = (probs * (prob_grad - inner_sum)).astype(jnp.bfloat16)
        query_grads.append(
            jnp.einsum(
                "hqk,khd->qhd", score_grad, key_rows[:stop_row], preferred_element_type=jnp.float32
            )
            * scaling
        )
        key_grad = key_grad.at[:stop_row].add(
            jnp.einsum(
                "hqk,qhd->khd",
                score_grad,
                queries[start_row:stop_row],
                preferred_element_type=jnp.float32,
            )
            * scaling
        )
        value_grad = value_grad.at[:stop_row].add(
            jnp.einsum(
                "hqk,qhd->khd",
                probs.astype(jnp.bfloat16),
                grad_here,
                preferred_element_type=jnp.float32,
            )
        )
    return (jnp.concatenate(query_grads, 0), key_grad, value_grad)


def merge_stats(first, second):
    top_score = jnp.maximum(first[0], second[0])
    row_total = first[1] * jnp.exp(first[0] - top_score) + second[1] * jnp.exp(
        second[0] - top_score
    )
    return (top_score, row_total, first[2] + second[2])


def per_device(
    token_ids,
    prompt_len,
    example_len,
    embedding,
    w_qkv,
    w_out,
    w_in,
    b_in,
    w_down,
    unembed,
    ln_gain,
    ln_bias,
    master,
    first_moment,
    second_moment,
    eigen_bases,
):
    group_count = lax.axis_size("mp")
    group_index = lax.axis_index("mp")
    adapters = lax.all_gather(master.astype(jnp.bfloat16), ("dp", "mp"), axis=1, tiled=True)
    head_local = lax.all_gather(unembed, "dp", axis=0, tiled=True)
    examples, length = token_ids.shape
    width = embedding.shape[0]
    vocab_local = head_local.shape[1]
    rows = examples * length
    local_heads = HEADS // group_count
    group_width = local_heads * HD
    flat_ids = token_ids.reshape(rows)
    relative = flat_ids - group_index * width
    inside = (relative >= 0) & (relative < width)
    picked = jnp.where(
        inside[:, None], embedding[jnp.clip(relative, 0, width - 1)].astype(jnp.float32), 0.0
    )
    start_rows = lax.psum(picked.astype(jnp.bfloat16), "mp").astype(jnp.float32)
    leading_example = lax.axis_index("dp") * examples
    prompts = lax.dynamic_slice_in_dim(prompt_len, leading_example, examples)
    totals = lax.dynamic_slice_in_dim(example_len, leading_example, examples)
    position = jnp.arange(length)
    keep = (position[None, :] >= prompts[:, None] - 1) & (position[None, :] < totals[:, None] - 1)
    count = jnp.sum(example_len - prompt_len).astype(jnp.float32)
    row_weight = keep.reshape(rows).astype(jnp.float32) / count
    target = jnp.roll(token_ids, -1, axis=1).reshape(rows)
    normed_attn = layer_norm(start_rows, ln_gain[0], ln_bias[0]).astype(jnp.bfloat16)
    normed_ffn = layer_norm(start_rows, ln_gain[1], ln_bias[1]).astype(jnp.bfloat16)
    inner = jnp.dot(
        normed_attn,
        jnp.concatenate([adapters[0], adapters[1], adapters[2]], 1),
        preferred_element_type=jnp.float32,
    ).astype(jnp.bfloat16)
    base = jnp.dot(normed_attn, w_qkv, preferred_element_type=jnp.float32).reshape(
        rows, local_heads, 3, HD
    )
    adapter_rows = [
        lax.dynamic_slice_in_dim(
            adapters[3 + selector_index], group_index * group_width, group_width, 0
        )
        for selector_index in range(3)
    ]
    pre_parts = []
    for selector_index in range(3):
        extra = jnp.einsum(
            "lr,dr->ld",
            inner[:, selector_index * R : (selector_index + 1) * R],
            adapter_rows[selector_index],
            preferred_element_type=jnp.float32,
        )
        pre_parts.append(base[:, :, selector_index] + extra.reshape(rows, local_heads, HD))
    cosine, sine = rope_tables(length)
    queries = rotate(pre_parts[0].reshape(examples, length, local_heads, HD), cosine, sine).astype(
        jnp.bfloat16
    )
    key_rows = rotate(pre_parts[1].reshape(examples, length, local_heads, HD), cosine, sine).astype(
        jnp.bfloat16
    )
    value_rows = pre_parts[2].reshape(examples, length, local_heads, HD).astype(jnp.bfloat16)
    sample = 0
    context_here, spread_local = attend(queries[sample], key_rows[sample], value_rows[sample])
    spreads = [spread_local]
    context = context_here.reshape(rows, group_width)
    out_rows = lax.dynamic_slice_in_dim(adapters[6], group_index * group_width, group_width, 0)
    inner_out = jnp.dot(context, out_rows, preferred_element_type=jnp.float32).astype(jnp.bfloat16)
    hidden = jax.nn.gelu(
        jnp.dot(normed_ffn, w_in, preferred_element_type=jnp.float32) + b_in, approximate=False
    ).astype(jnp.bfloat16)
    partial_value = (
        jnp.dot(context, w_out, preferred_element_type=jnp.float32)
        + jnp.einsum("lr,dr->ld", inner_out, adapters[7], preferred_element_type=jnp.float32)
        + jnp.dot(hidden, w_down, preferred_element_type=jnp.float32)
    )
    resid = start_rows + lax.psum(partial_value, "mp")
    final_rows = layer_norm(resid, ln_gain[2], ln_bias[2]).astype(jnp.bfloat16)
    row_block = min(256, rows)
    blocks = rows // row_block
    vocab_ids = jnp.arange(vocab_local)[None, :]

    def block_stats(pieces):
        rows_here, target_here = pieces
        logits = jnp.dot(rows_here, head_local, preferred_element_type=jnp.float32)
        top_score = jnp.max(logits, -1)
        row_total = jnp.sum(jnp.exp(logits - top_score[:, None]), -1)
        hit = vocab_ids == (target_here - group_index * vocab_local)[:, None]
        return (top_score, row_total, jnp.sum(jnp.where(hit, logits, 0.0), -1))

    stats = lax.map(
        block_stats, (final_rows.reshape(blocks, row_block, D), target.reshape(blocks, row_block))
    )
    top_score, row_total, target_logit = merged(
        (stats[0].reshape(rows), stats[1].reshape(rows), stats[2].reshape(rows)), "mp", merge_stats
    )
    spread_all = top_score + jnp.log(row_total)
    local_loss = jnp.sum((spread_all - target_logit) * row_weight)

    def block_back(pieces):
        rows_here, target_here, spread_local, weight_here = pieces
        logits = jnp.dot(rows_here, head_local, preferred_element_type=jnp.float32)
        hit = (vocab_ids == (target_here - group_index * vocab_local)[:, None]).astype(jnp.float32)
        logit_grad = (
            (jnp.exp(logits - spread_local[:, None]) - hit) * weight_here[:, None]
        ).astype(jnp.bfloat16)
        return jnp.einsum("lv,dv->ld", logit_grad, head_local, preferred_element_type=jnp.float32)

    head_grad = lax.map(
        block_back,
        (
            final_rows.reshape(blocks, row_block, D),
            target.reshape(blocks, row_block),
            spread_all.reshape(blocks, row_block),
            row_weight.reshape(blocks, row_block),
        ),
    ).reshape(rows, D)
    branch_grad = norm_back(resid, ln_gain[2], ln_bias[2], lax.psum(head_grad, "mp")).astype(
        jnp.bfloat16
    )
    inner_out_grad = jnp.dot(branch_grad, adapters[7], preferred_element_type=jnp.float32).astype(
        jnp.bfloat16
    )
    grad_out_b = jnp.einsum("ld,lr->dr", branch_grad, inner_out, preferred_element_type=jnp.float32)
    grad_out_a = jnp.einsum(
        "ld,lr->dr", context, inner_out_grad, preferred_element_type=jnp.float32
    )
    context_grad = jnp.einsum(
        "ld,ed->le", branch_grad, w_out, preferred_element_type=jnp.float32
    ) + jnp.einsum("lr,dr->ld", inner_out_grad, out_rows, preferred_element_type=jnp.float32)
    context_grad = context_grad.astype(jnp.bfloat16).reshape(examples, length, local_heads, HD)
    sample = 0
    query_grad, key_grad, value_grad = attend_back(
        queries[sample], key_rows[sample], value_rows[sample], spreads[sample], context_grad[sample]
    )
    query_parts = [rotate_back(query_grad, cosine, sine)]
    key_parts = [rotate_back(key_grad, cosine, sine)]
    value_parts = [value_grad]
    pre_grads = [
        parts[0].reshape(rows, group_width).astype(jnp.bfloat16)
        for parts in (query_parts, key_parts, value_parts)
    ]
    complete_gradients = []
    local_grads = []
    for selector_index in range(3):
        projected_values = jnp.einsum(
            "ld,le->de", normed_attn, pre_grads[selector_index], preferred_element_type=jnp.float32
        )
        complete_gradients.append(
            jnp.dot(
                projected_values,
                adapter_rows[selector_index].astype(jnp.float32),
                precision=HIGH_PRECISION,
            )
        )
        local_grads.append(
            jnp.einsum(
                "ld,lr->dr",
                pre_grads[selector_index],
                inner[:, selector_index * R : (selector_index + 1) * R],
                preferred_element_type=jnp.float32,
            )
        )
    local_grads.append(grad_out_a)
    placed = lax.dynamic_update_slice(
        jnp.zeros((4, D, R), jnp.float32), jnp.stack(local_grads), (0, group_index * group_width, 0)
    )
    gradient = jnp.concatenate([jnp.stack(complete_gradients), placed, grad_out_b[None]], 0)
    owned = lax.psum_scatter(gradient, ("dp", "mp"), scatter_dimension=1, tiled=True)
    squares = jnp.sum(owned * owned)
    norm_squared = lax.psum(squares, ("dp", "mp"))
    mean_loss = lax.psum(local_loss, "dp")
    grad_norm = jnp.sqrt(norm_squared)
    clipped = owned * jnp.minimum(1.0, CLIP_LIMIT / grad_norm)
    rotated = jnp.einsum("mdr,mrs->mds", clipped, eigen_bases, precision=HIGH_PRECISION)
    new_first = BETA_FIRST * first_moment + (1.0 - BETA_FIRST) * rotated
    new_second = BETA_SECOND * second_moment + (1.0 - BETA_SECOND) * rotated * rotated
    normed = (
        new_first
        / (1.0 - BETA_FIRST**ADAM_STEP)
        / (jnp.sqrt(new_second / (1.0 - BETA_SECOND**ADAM_STEP)) + ADAM_EPS)
    )
    turned = jnp.einsum("mds,mrs->mdr", normed, eigen_bases, precision=HIGH_PRECISION)
    new_master = master - LEARN_RATE * (turned + DECAY_RATE * master)
    return (mean_loss, grad_norm, new_first, new_second, new_master)


def solution(mesh):
    placed = (
        P("dp", None),
        P(),
        P(),
        P("mp", None),
        P(None, "mp"),
        P("mp", None),
        P(None, "mp"),
        P("mp"),
        P("mp", None),
        P("dp", "mp"),
        P(),
        P(),
        P(None, ("dp", "mp"), None),
        P(None, ("dp", "mp"), None),
        P(None, ("dp", "mp"), None),
        P(),
    )
    return jax.shard_map(
        per_device,
        mesh=mesh,
        in_specs=placed,
        out_specs=(
            P(),
            P(),
            P(None, ("dp", "mp"), None),
            P(None, ("dp", "mp"), None),
            P(None, ("dp", "mp"), None),
        ),
        check_vma=False,
    )
```

profile of v0, /device:TPU:14, one launch (start us, length us, event | category | flops | bytes accessed | tf_op | source)
XLA Modules:
  0.0 1017.0 jit_solution(3470732560925565724)
XLA Ops:
  9.6 17.7 %gather_fusion = bf16[1024,1024]{1,0:T(8,128)(2,1)} fusion(bf16[12576,1024]{1,0:T(8,128)(2,1)} %param.37, s32[1024]{0:T(1024)S(1)} %broadcast_clamp_fusion), kind=kCustom, calls=%fused_computation | custom fusion | bytes 4198400 | tf_op jit(solution)/shard_map/gather | solution.py:183
  32.3 87.9 %all-reduce.6.cloned.1.call-done = bf16[1024,1024]{1,0:T(8,128)(2,1)} async-done(((bf16[1024,1024]{1,0:T(8,128)(2,1)}), bf16[1024,1024]{1,0:T(8,128)(2,1)}) %all-reduce.6.cloned.1.call-update) | async-done | bytes 2097168 | tf_op jit(solution)/shard_map/psum | solution.py:185
  129.1 16.4 %fusion.56 = f32[1024,1024]{1,0:T(8,128)} fusion(bf16[1024,1024]{1,0:T(8,128)(2,1)S(1)} %copy-done, f32[1024]{0:T(1024)S(1)} %copy-done.75, bf16[1024,1024]{1,0:T(8,128)(2,1)} %param.40, bf16[1024,1024]{1,0:T(8,128)(2,1)} %all-reduce.6.cloned.1.call-done, f32[1024]{0:T(1024)S(1)} %bitcast.338, f32[1024]{0:T(1024)S(1)} %bitcast.337, ...), kind=kOutput, calls=%fused_computation.95 | convolution fusion | flops 4370464768 | bytes 10506240 | tf_op jit(solution)/shard_map/dot_general | solution.py:239
  179.2 142.3 %all-reduce.8.cloned.1.call-done = f32[1024,1024]{1,0:T(8,128)} async-done(((f32[1024,1024]{1,0:T(8,128)}), f32[1024,1024]{1,0:T(8,128)}) %all-reduce.8.cloned.1.call-update) | async-done | bytes 4194320 | tf_op jit(solution)/shard_map/psum | solution.py:241
  328.2 102.9 %while.54 = (s32[]{:T(128)}, f32[4,256]{1,0:T(4,128)S(1)}, f32[4,256]{1,0:T(4,128)S(1)}, f32[4,256]{1,0:T(4,128)S(1)}, bf16[4,256,1024]{2,1,0:T(8,128)(2,1)}, /*...) while((s32[]{:T(128)}, f32[4,256]{1,0:T(4,128)S(1)}, ...), condition=%wide.region_14.15_spmd.clone.clone, body=%wide.region_10.14_spmd.clone.sunk.clone | while | flops 6612762112 | bytes 52246120 | solution.py:255
  328.2 18.8 %fusion.255 = (f32[256]{0:T(256)S(1)}, f32[256,12576]{0,1:T(8,128)}) fusion(bf16[1024,12576]{1,0:T(8,128)(2,1)} %get-tuple-element.709, bf16[4,256,1024]{2,1,0:T(8,128)(2,1)} %get-tuple-element.708, s32[]{:T(128)} %get-tuple-element.696), kind=kOutput, calls=%fused_computation.294.clone.1.clone | convolution fusion | flops 6596665344 | bytes 39355904 | tf_op jit(solution)/shard_map/while/body/eval_jaxpr/dot_general | solution.py:249
  354.0 18.9 %fusion.255 = (f32[256]{0:T(256)S(1)}, f32[256,12576]{0,1:T(8,128)}) fusion(bf16[1024,12576]{1,0:T(8,128)(2,1)} %get-tuple-element.709, bf16[4,256,1024]{2,1,0:T(8,128)(2,1)} %get-tuple-element.708, s32[]{:T(128)} %get-tuple-element.696), kind=kOutput, calls=%fused_computation.294.clone.1.clone | convolution fusion | flops 6596665344 | bytes 39355904 | tf_op jit(solution)/shard_map/while/body/eval_jaxpr/dot_general | solution.py:249
  372.9 6.7 select_reduce_fusion.3
  379.7 18.9 %fusion.255 = (f32[256]{0:T(256)S(1)}, f32[256,12576]{0,1:T(8,128)}) fusion(bf16[1024,12576]{1,0:T(8,128)(2,1)} %get-tuple-element.709, bf16[4,256,1024]{2,1,0:T(8,128)(2,1)} %get-tuple-element.708, s32[]{:T(128)} %get-tuple-element.696), kind=kOutput, calls=%fused_computation.294.clone.1.clone | convolution fusion | flops 6596665344 | bytes 39355904 | tf_op jit(solution)/shard_map/while/body/eval_jaxpr/dot_general | solution.py:249
  398.6 6.7 select_reduce_fusion.3
  405.5 18.8 %fusion.255 = (f32[256]{0:T(256)S(1)}, f32[256,12576]{0,1:T(8,128)}) fusion(bf16[1024,12576]{1,0:T(8,128)(2,1)} %get-tuple-element.709, bf16[4,256,1024]{2,1,0:T(8,128)(2,1)} %get-tuple-element.708, s32[]{:T(128)} %get-tuple-element.696), kind=kOutput, calls=%fused_computation.294.clone.1.clone | convolution fusion | flops 6596665344 | bytes 39355904 | tf_op jit(solution)/shard_map/while/body/eval_jaxpr/dot_general | solution.py:249
  424.3 6.7 select_reduce_fusion.3
  431.2 13.2 %all-gather = f32[4,1,1024]{2,1,0:T(1,128)S(1)} all-gather(f32[1,1,1024]{2,1,0:T(1,128)S(1)} %reshape.547), channel_id=1, replica_groups=mesh['dp'=8,'mp'=4] {'mp'}, dimensions={0}, use_global_device_ids=true | all-gather | bytes 20480 | tf_op jit(solution)/shard_map/all_gather | solution.py:24
  444.4 13.4 %all-gather.1 = f32[4,1,1024]{2,1,0:T(1,128)S(1)} all-gather(f32[1,1,1024]{2,1,0:T(1,128)S(1)} %reshape.549), channel_id=1, replica_groups=mesh['dp'=8,'mp'=4] {'mp'}, dimensions={0}, use_global_device_ids=true | all-gather | bytes 20480 | tf_op jit(solution)/shard_map/all_gather | solution.py:24
  457.8 13.2 %all-gather.2 = f32[4,1,1024]{2,1,0:T(1,128)S(1)} all-gather(f32[1,1,1024]{2,1,0:T(1,128)S(1)} %reshape.551), channel_id=1, replica_groups=mesh['dp'=8,'mp'=4] {'mp'}, dimensions={0}, use_global_device_ids=true | all-gather | bytes 20480 | tf_op jit(solution)/shard_map/all_gather | solution.py:24
  471.9 135.9 %while.55 = (s32[]{:T(128)}, f32[4,256,1024]{2,1,0:T(8,128)}, bf16[4,256,1024]{2,1,0:T(8,128)(2,1)}, bf16[1024,12576]{1,0:T(8,128)(2,1)}, f32[4,256]{1,0:T(4,128...) while((s32[]{:T(128)}, f32[4,256,1024]{2,1,0:T(8,128)}, ...), condition=%wide.region_21.22_spmd.clone.clone, body=%wide.region_20.21_spmd.clone.sunk.clone | while | flops 13206208512 | bytes 53487712 | solution.py:273
  471.9 34.0 %fusion.260 = f32[4,256,1024]{2,1,0:T(8,128)} fusion(f32[4,256,1024]{2,1,0:T(8,128)} %get-tuple-element.742, s32[]{:T(128)} %get-tuple-element.741, bf16[1024,12576]{1,0:T(8,128)(2,1)} %get-tuple-element.752, f32[256]{0:T(256)S(1)} %bitcast.331, s32[256]{0:T(256)S(1)} %bitcast.330, f32[256]{0:T(256)S(1)} %bitcast.332, ...), kind=kOutput, calls=%fused_computation.22.clone.1.clone | convolution fusion | flops 13206208512 | bytes 53481472 | tf_op jit(solution)/shard_map/while/body/eval_jaxpr/lv,dv->ld/dot_general | solution.py:271
  505.9 34.0 %fusion.260 = f32[4,256,1024]{2,1,0:T(8,128)} fusion(f32[4,256,1024]{2,1,0:T(8,128)} %get-tuple-element.742, s32[]{:T(128)} %get-tuple-element.741, bf16[1024,12576]{1,0:T(8,128)(2,1)} %get-tuple-element.752, f32[256]{0:T(256)S(1)} %bitcast.331, s32[256]{0:T(256)S(1)} %bitcast.330, f32[256]{0:T(256)S(1)} %bitcast.332, ...), kind=kOutput, calls=%fused_computation.22.clone.1.clone | convolution fusion | flops 13206208512 | bytes 53481472 | tf_op jit(solution)/shard_map/while/body/eval_jaxpr/lv,dv->ld/dot_general | solution.py:271
  539.9 33.9 %fusion.260 = f32[4,256,1024]{2,1,0:T(8,128)} fusion(f32[4,256,1024]{2,1,0:T(8,128)} %get-tuple-element.742, s32[]{:T(128)} %get-tuple-element.741, bf16[1024,12576]{1,0:T(8,128)(2,1)} %get-tuple-element.752, f32[256]{0:T(256)S(1)} %bitcast.331, s32[256]{0:T(256)S(1)} %bitcast.330, f32[256]{0:T(256)S(1)} %bitcast.332, ...), kind=kOutput, calls=%fused_computation.22.clone.1.clone | convolution fusion | flops 13206208512 | bytes 53481472 | tf_op jit(solution)/shard_map/while/body/eval_jaxpr/lv,dv->ld/dot_general | solution.py:271
  573.9 33.9 %fusion.260 = f32[4,256,1024]{2,1,0:T(8,128)} fusion(f32[4,256,1024]{2,1,0:T(8,128)} %get-tuple-element.742, s32[]{:T(128)} %get-tuple-element.741, bf16[1024,12576]{1,0:T(8,128)(2,1)} %get-tuple-element.752, f32[256]{0:T(256)S(1)} %bitcast.331, s32[256]{0:T(256)S(1)} %bitcast.330, f32[256]{0:T(256)S(1)} %bitcast.332, ...), kind=kOutput, calls=%fused_computation.22.clone.1.clone | convolution fusion | flops 13206208512 | bytes 53481472 | tf_op jit(solution)/shard_map/while/body/eval_jaxpr/lv,dv->ld/dot_general | solution.py:271
  608.5 153.3 %all-reduce.10.cloned.1.call-done = f32[1024,1024]{1,0:T(8,128)} async-done(((f32[1024,1024]{1,0:T(8,128)}), f32[1024,1024]{1,0:T(8,128)}) %all-reduce.10.cloned.1.call-update) | async-done | bytes 4194320 | tf_op jit(solution)/shard_map/psum | solution.py:282
  799.6 140.3 %reduce-scatter.2.cloned.1.call-done = f32[8,32,128]{2,1,0:T(8,128)} async-done(((f32[8,1024,128]{2,1,0:T(8,128)}), f32[8,32,128]{2,1,0:T(8,128)}) %reduce-scatter.2.cloned.1.call-update) | async-done | bytes 131088 | tf_op jit(solution)/shard_map/reduce_scatter | solution.py:333
  941.4 18.1 %psum.37 = f32[]{:T(128)} all-reduce(f32[]{:T(128)} %get-tuple-element.415), channel_id=1, replica_groups=mesh['dp'=8,'mp'=4] {'dp'}, use_global_device_ids=true, to_apply=%region_19.20 | all-reduce | flops 1 | bytes 8 | tf_op jit(solution)/shard_map/psum | solution.py:336
  959.5 44.9 %psum.39 = f32[]{:T(128)} all-reduce(f32[]{:T(128)} %multiply_reduce_fusion.4), channel_id=1, replica_groups=mesh['dp'=8,'mp'=4] {'dp','mp'}, use_global_device_ids=true, to_apply=%region_29.30 | all-reduce | flops 1 | bytes 8 | tf_op jit(solution)/shard_map/psum | solution.py:335
  (327 shorter events, 104.0 us)
Async XLA Ops:
  8.0 121.1 %copy-start = (bf16[1024,1024]{1,0:T(8,128)(2,1)S(1)}, bf16[1024,1024]{1,0:T(8,128)(2,1)}, u32[]{:S(2)}) copy-start(bf16[1024,1024]{1,0:T(8,128)(2,1)} %param.42) | copy-start | bytes 6291460
  8.0 112.2 %all-reduce.6.cloned.1.call-start = ((), (), s32[]{:S(2)}) async-start(), calls=%async_computation.1 | async-start | bytes 4194304 | tf_op jit(solution)/shard_map/psum | solution.py:185
  30.7 114.7 %all-gather.6.cloned.1.call-start = ((), (), s32[]{:S(2)}) async-start(), calls=%async_computation.2 | async-start | bytes 2162688 | tf_op jit(solution)/shard_map/all_gather | solution.py:171
  31.5 290.1 %all-reduce.8.cloned.1.call-start = ((), (), s32[]{:S(2)}) async-start(), calls=%async_computation.3 | async-start | bytes 8388608 | tf_op jit(solution)/shard_map/psum | solution.py:241
  31.7 294.2 %copy-start.57 = (f32[1,1024]{1,0:T(1,128)}, f32[1,1024]{1,0:T(1,128)S(1)}, u32[]{:S(2)}) copy-start(f32[1,1024]{1,0:T(1,128)S(1)} %get-tuple-element.447) | copy-start | bytes 12292
  31.9 119.4 %copy-start.45 = (f32[1024,8]{0,1:T(8,128)}, f32[1024,8]{0,1:T(8,128)S(1)}, u32[]{:S(2)}) copy-start(f32[1024,8]{0,1:T(8,128)S(1)} %get-tuple-element.452) | copy-start | bytes 98308
  31.9 119.4 %copy-start.47 = (f32[1024,8]{0,1:T(8,128)}, f32[1024,8]{0,1:T(8,128)S(1)}, u32[]{:S(2)}) copy-start(f32[1024,8]{0,1:T(8,128)S(1)} %get-tuple-element.453) | copy-start | bytes 98308
  147.0 14.4 %copy-start.44 = (bf16[1,1024,128]{2,1,0:T(8,128)(2,1)}, bf16[1,1024,128]{2,1,0:T(8,128)(2,1)S(1)}, u32[]{:S(2)}) copy-start(bf16[1,1024,128]{2,1,0:T(8,128)(2,1)S(1)} %get-tuple-element.423) | copy-start | bytes 786436
  151.3 9.3 copy-start.14
  167.9 8.1 copy-start.76
  167.9 153.6 %copy-start.4 = (bf16[1024,1024]{1,0:T(8,128)(2,1)S(1)}, bf16[1024,1024]{1,0:T(8,128)(2,1)}, u32[]{:S(2)}) copy-start(bf16[1024,1024]{1,0:T(8,128)(2,1)} %all-reduce.6.cloned.1.call-done) | copy-start | bytes 6291460
  168.0 160.3 %all-gather.8.cloned.1.call-start = ((), (), s32[]{:S(2)}) async-start(), calls=%async_computation.4 | async-start | bytes 29196288 | tf_op jit(solution)/shard_map/all_gather | solution.py:172
  173.8 588.1 %all-reduce.10.cloned.1.call-start = ((), (), s32[]{:S(2)}) async-start(), calls=%async_computation.5 | async-start | bytes 8388608 | tf_op jit(solution)/shard_map/psum | solution.py:282
  607.8 154.1 %copy-start.5 = (bf16[1024,1024]{1,0:T(8,128)(2,1)S(1)}, bf16[1024,1024]{1,0:T(8,128)(2,1)}, u32[]{:S(2)}) copy-start(bf16[1024,1024]{1,0:T(8,128)(2,1)} %all-reduce.6.cloned.1.call-done) | copy-start | bytes 6291460
  607.8 154.1 %copy-start.56 = (f32[1024]{0:T(1024)S(1)}, f32[1024]{0:T(1024)}, u32[]{:S(2)}) copy-start(f32[1024]{0:T(1024)} %copy-done.55) | copy-start | bytes 12292
  607.8 154.1 %copy-start.58 = (f32[1,1024]{1,0:T(1,128)S(1)}, f32[1,1024]{1,0:T(1,128)}, u32[]{:S(2)}) copy-start(f32[1,1024]{1,0:T(1,128)} %copy-done.57) | copy-start | bytes 12292
  607.8 332.0 %reduce-scatter.2.cloned.1.call-start = ((), (), s32[]{:S(2)}) async-start(), calls=%async_computation.6 | async-start | bytes 4325376 | tf_op jit(solution)/shard_map/reduce_scatter | solution.py:333
  608.5 158.0 %copy-start.62 = (f32[1024]{0:T(1024)S(1)}, f32[1024]{0:T(1024)}, u32[]{:S(2)}) copy-start(f32[1024]{0:T(1024)} %copy-done.61) | copy-start | bytes 12292
  608.5 158.0 %copy-start.60 = (f32[1024]{0:T(1024)S(1)}, f32[1024]{0:T(1024)}, u32[]{:S(2)}) copy-start(f32[1024]{0:T(1024)} %copy-done.59) | copy-start | bytes 12292
  798.0 207.2 %copy-start.23 = (f32[8,128,128]{2,1,0:T(8,128)S(1)}, f32[8,128,128]{2,1,0:T(8,128)}, u32[]{:S(2)}) copy-start(f32[8,128,128]{2,1,0:T(8,128)} %param.49) | copy-start | bytes 1572868
  798.0 207.2 %copy-start.53 = (f32[8,32,128]{2,1,0:T(8,128)S(1)}, f32[8,32,128]{2,1,0:T(8,128)}, u32[]{:S(2)}) copy-start(f32[8,32,128]{2,1,0:T(8,128)} %param.48) | copy-start | bytes 393220
  798.0 207.2 %copy-start.54 = (f32[8,32,128]{2,1,0:T(8,128)S(1)}, f32[8,32,128]{2,1,0:T(8,128)}, u32[]{:S(2)}) copy-start(f32[8,32,128]{2,1,0:T(8,128)} %param.47) | copy-start | bytes 393220
  798.0 208.7 %copy-start.43 = (f32[8,32,128]{2,1,0:T(8,128)S(1)}, f32[8,32,128]{2,1,0:T(8,128)}, u32[]{:S(2)}) copy-start(f32[8,32,128]{2,1,0:T(8,128)} %param.46) | copy-start | bytes 393220
  798.0 210.3 %copy-start.1 = (bf16[1024,1024]{1,0:T(8,128)(2,1)S(1)}, bf16[1024,1024]{1,0:T(8,128)(2,1)}, u32[]{:S(2)}) copy-start(bf16[1024,1024]{1,0:T(8,128)(2,1)} %param.42) | copy-start | bytes 6291460
  (62 other events, 168.4 us)
Sparse Core Ops, SparseCore 0:
  30.9 89.3 all-reduce.5
  168.0 153.4 all-reduce.7
  608.0 153.8 all-reduce.9
Sparse Core Ops, SparseCore 1:
  34.7 98.1 all-gather.5
  173.9 127.9 all-gather.7
  799.7 140.1 reduce-scatter.1
where the time goes:
time: 1020 us
  waiting for transfers between devices  524 us (51%)
  matrix products  271 us (27%)
  blocking collectives  103 us (10%)
  other arithmetic  61.3 us (6%)
  local copies, waits for them, and re-layouts  36.2 us (4%)
  between operations  20.9 us (2%)
    psum x1, waiting for transfers between devices, per_device(): lax.psum(head_grad, 'mp')  153 us
    psum x1, waiting for transfers between devices, per_device(): resid = start_rows + lax.psum(partial_value, 'mp')  142 us
    reduce_scatter x1, waiting for transfers between devices, per_device(): lax.psum_scatter(gradient, ('dp', 'mp'), scatter_dimension=1, tiled=True)  140 us
    dot_general x4, matrix products, block_back(): jnp.einsum('lv,dv->ld', logit_grad, head_local, preferred_element_type=jn...  136 us
    psum x1, waiting for transfers between devices, per_device(): start_rows = lax.psum(picked.astype(jnp.bfloat16), 'mp').astype(jnp.float32)  87.9 us
    dot_general x4, matrix products, block_stats(): logits = jnp.dot(rows_here, head_local, preferred_element_type=jnp.float32)  75.4 us
    psum x1, blocking collectives, per_device(): norm_squared = lax.psum(squares, ('dp', 'mp'))  44.9 us
    all_gather x3, blocking collectives, merged(): pieces = jax.tree.map(lambda part: lax.all_gather(part, axis), value)  39.8 us
  transfers between devices with their start and end apart: 6, of which 4 were waited for; matrix products, arithmetic and copies ran while one was open for 4% of the time, Pallas kernels for 0%

commit v1 on v0

--- a/solution.py
+++ b/solution.py
@@ -238,7 +238,7 @@
         + jnp.einsum("lr,dr->ld", inner_out, adapters[7], preferred_element_type=jnp.float32)
         + jnp.dot(hidden, w_down, preferred_element_type=jnp.float32)
     )
-    resid = start_rows + lax.psum(partial_value, "mp")
+    resid = start_rows + jnp.sum(lax.all_gather(partial_value, "mp"), axis=0)
     final_rows = layer_norm(resid, ln_gain[2], ln_bias[2]).astype(jnp.bfloat16)
     row_block = min(256, rows)
     blocks = rows // row_block

time: 1020 us -> 1280 us (1.25)
  waiting for transfers between devices: 524 us -> 767 us
    all_gather x0 -> x1, waiting for transfers between devices: none -> 274 us  [per_device(): resid = start_rows + jnp.sum(lax.all_gather(partial_value, 'mp'), axis=0)]
    psum x1 -> x0, waiting for transfers between devices: 142 us -> none  [per_device(): resid = start_rows + lax.psum(partial_value, 'mp')]
    all_gather x1, waiting for transfers between devices: 0.01 us -> 112 us  [per_device(): head_local = lax.all_gather(unembed, 'dp', axis=0, tiled=True)]
  transfers between devices with their start and end apart: 6 -> 6, of which waited for: 4 -> 5; matrix products, arithmetic and copies ran while one was open for 4% -> 4% of each run, Pallas kernels for 0% -> 0%
where the time goes in v1:
time: 1280 us; the launch traced here: 1270 us
  waiting for transfers between devices  767 us (60%)
  matrix products  271 us (21%)
  blocking collectives  102 us (8%)
  other arithmetic  72.8 us (6%)
  local copies, waits for them, and re-layouts  36.4 us (3%)
  between operations  20.8 us (2%)
    all_gather x1, waiting for transfers between devices, per_device(): resid = start_rows + jnp.sum(lax.all_gather(partial_value, 'mp'), axis=0)  274 us
    psum x1, waiting for transfers between devices, per_device(): lax.psum(head_grad, 'mp')  153 us
    reduce_scatter x1, waiting for transfers between devices, per_device(): lax.psum_scatter(gradient, ('dp', 'mp'), scatter_dimension=1, tiled=True)  141 us
    dot_general x4, matrix products, block_back(): jnp.einsum('lv,dv->ld', logit_grad, head_local, preferred_element_type=jn...  136 us
    all_gather x1, waiting for transfers between devices, per_device(): head_local = lax.all_gather(unembed, 'dp', axis=0, tiled=True)  112 us
    psum x1, waiting for transfers between devices, per_device(): start_rows = lax.psum(picked.astype(jnp.bfloat16), 'mp').astype(jnp.float32)  87.9 us
    dot_general x4, matrix products, block_stats(): logits = jnp.dot(rows_here, head_local, preferred_element_type=jnp.float32)  75.4 us
    psum x1, blocking collectives, per_device(): norm_squared = lax.psum(squares, ('dp', 'mp'))  45 us
  transfers between devices with their start and end apart: 6, of which 5 were waited for; matrix products, arithmetic and copies ran while one was open for 4% of the time, Pallas kernels for 0%

profile of v1, /device:TPU:14, one launch (start us, length us, event | category | flops | bytes accessed | tf_op | source)
XLA Modules:
  0.0 1271.0 jit_solution(9383689643281692479)
XLA Ops:
  9.6 17.7 %gather_fusion = bf16[1024,1024]{1,0:T(8,128)(2,1)} fusion(bf16[12576,1024]{1,0:T(8,128)(2,1)} %param.37, s32[1024]{0:T(1024)S(1)} %broadcast_clamp_fusion), kind=kCustom, calls=%fused_computation | custom fusion | bytes 4198400 | tf_op jit(solution)/shard_map/gather | solution.py:183
  32.3 87.9 %all-reduce.5.cloned.1.call-done = bf16[1024,1024]{1,0:T(8,128)(2,1)} async-done(((bf16[1024,1024]{1,0:T(8,128)(2,1)}), bf16[1024,1024]{1,0:T(8,128)(2,1)}) %all-reduce.5.cloned.1.call-update) | async-done | bytes 2097168 | tf_op jit(solution)/shard_map/psum | solution.py:185
  129.1 16.5 %fusion.56 = f32[1024,1024]{1,0:T(8,128)} fusion(bf16[1024,1024]{1,0:T(8,128)(2,1)S(1)} %copy-done, f32[1024]{0:T(1024)S(1)} %copy-done.75, bf16[1024,1024]{1,0:T(8,128)(2,1)} %param.40, bf16[1024,1024]{1,0:T(8,128)(2,1)} %all-reduce.5.cloned.1.call-done, f32[1024]{0:T(1024)S(1)} %bitcast.340, f32[1024]{0:T(1024)S(1)} %bitcast.339, ...), kind=kOutput, calls=%fused_computation.95 | convolution fusion | flops 4370464768 | bytes 10506240 | tf_op jit(solution)/shard_map/dot_general | solution.py:239
  178.9 273.5 %all-gather.12.cloned.1.call-done = f32[4096,1024]{1,0:T(8,128)} async-done(((f32[1024,1024]{1,0:T(8,128)}), f32[4096,1024]{1,0:T(8,128)}) %all-gather.12.cloned.1.call-update) | async-done | bytes 16777232 | tf_op jit(solution)/shard_map/all_gather | solution.py:241
  452.5 10.8 reduce_sum.176
  471.2 111.7 %all-gather.10.cloned.1.call-done = bf16[1024,12576]{1,0:T(8,128)(2,1)} async-done(((bf16[128,12576]{1,0:T(8,128)(2,1)}), bf16[1024,12576]{1,0:T(8,128)(2,1)}) %all-gather.10.cloned.1.call-update) | async-done | bytes 25755664 | tf_op jit(solution)/shard_map/all_gather | solution.py:172
  582.9 103.0 %while.54 = (s32[]{:T(128)}, f32[4,256]{1,0:T(4,128)S(1)}, f32[4,256]{1,0:T(4,128)S(1)}, f32[4,256]{1,0:T(4,128)S(1)}, bf16[4,256,1024]{2,1,0:T(8,128)(2,1)}, /*...) while((s32[]{:T(128)}, f32[4,256]{1,0:T(4,128)S(1)}, ...), condition=%wide.region_14.15_spmd.clone.clone, body=%wide.region_10.14_spmd.clone.sunk.clone | while | flops 6612762112 | bytes 52246120 | solution.py:255
  583.1 18.8 %fusion.255 = (f32[256]{0:T(256)S(1)}, f32[256,12576]{0,1:T(8,128)}) fusion(bf16[1024,12576]{1,0:T(8,128)(2,1)} %get-tuple-element.709, bf16[4,256,1024]{2,1,0:T(8,128)(2,1)} %get-tuple-element.708, s32[]{:T(128)} %get-tuple-element.696), kind=kOutput, calls=%fused_computation.294.clone.1.clone | convolution fusion | flops 6596665344 | bytes 39355904 | tf_op jit(solution)/shard_map/while/body/eval_jaxpr/dot_general | solution.py:249
  601.9 6.7 select_reduce_fusion.3
  608.8 18.8 %fusion.255 = (f32[256]{0:T(256)S(1)}, f32[256,12576]{0,1:T(8,128)}) fusion(bf16[1024,12576]{1,0:T(8,128)(2,1)} %get-tuple-element.709, bf16[4,256,1024]{2,1,0:T(8,128)(2,1)} %get-tuple-element.708, s32[]{:T(128)} %get-tuple-element.696), kind=kOutput, calls=%fused_computation.294.clone.1.clone | convolution fusion | flops 6596665344 | bytes 39355904 | tf_op jit(solution)/shard_map/while/body/eval_jaxpr/dot_general | solution.py:249
  634.5 18.9 %fusion.255 = (f32[256]{0:T(256)S(1)}, f32[256,12576]{0,1:T(8,128)}) fusion(bf16[1024,12576]{1,0:T(8,128)(2,1)} %get-tuple-element.709, bf16[4,256,1024]{2,1,0:T(8,128)(2,1)} %get-tuple-element.708, s32[]{:T(128)} %get-tuple-element.696), kind=kOutput, calls=%fused_computation.294.clone.1.clone | convolution fusion | flops 6596665344 | bytes 39355904 | tf_op jit(solution)/shard_map/while/body/eval_jaxpr/dot_general | solution.py:249
  660.2 18.9 %fusion.255 = (f32[256]{0:T(256)S(1)}, f32[256,12576]{0,1:T(8,128)}) fusion(bf16[1024,12576]{1,0:T(8,128)(2,1)} %get-tuple-element.709, bf16[4,256,1024]{2,1,0:T(8,128)(2,1)} %get-tuple-element.708, s32[]{:T(128)} %get-tuple-element.696), kind=kOutput, calls=%fused_computation.294.clone.1.clone | convolution fusion | flops 6596665344 | bytes 39355904 | tf_op jit(solution)/shard_map/while/body/eval_jaxpr/dot_general | solution.py:249
  686.0 13.3 %all-gather.1 = f32[4,1,1024]{2,1,0:T(1,128)S(1)} all-gather(f32[1,1,1024]{2,1,0:T(1,128)S(1)} %reshape.548), channel_id=1, replica_groups=mesh['dp'=8,'mp'=4] {'mp'}, dimensions={0}, use_global_device_ids=true | all-gather | bytes 20480 | tf_op jit(solution)/shard_map/all_gather | solution.py:24
  699.2 13.2 %all-gather.2 = f32[4,1,1024]{2,1,0:T(1,128)S(1)} all-gather(f32[1,1,1024]{2,1,0:T(1,128)S(1)} %reshape.550), channel_id=1, replica_groups=mesh['dp'=8,'mp'=4] {'mp'}, dimensions={0}, use_global_device_ids=true | all-gather | bytes 20480 | tf_op jit(solution)/shard_map/all_gather | solution.py:24
  712.5 13.2 %all-gather.3 = f32[4,1,1024]{2,1,0:T(1,128)S(1)} all-gather(f32[1,1,1024]{2,1,0:T(1,128)S(1)} %reshape.552), channel_id=1, replica_groups=mesh['dp'=8,'mp'=4] {'mp'}, dimensions={0}, use_global_device_ids=true | all-gather | bytes 20480 | tf_op jit(solution)/shard_map/all_gather | solution.py:24
  726.6 135.8 %while.55 = (s32[]{:T(128)}, f32[4,256,1024]{2,1,0:T(8,128)}, bf16[4,256,1024]{2,1,0:T(8,128)(2,1)}, bf16[1024,12576]{1,0:T(8,128)(2,1)}, f32[4,256]{1,0:T(4,128...) while((s32[]{:T(128)}, f32[4,256,1024]{2,1,0:T(8,128)}, ...), condition=%wide.region_21.22_spmd.clone.clone, body=%wide.region_20.21_spmd.clone.sunk.clone | while | flops 13206208512 | bytes 53487712 | solution.py:273
  726.6 33.9 %fusion.260 = f32[4,256,1024]{2,1,0:T(8,128)} fusion(f32[4,256,1024]{2,1,0:T(8,128)} %get-tuple-element.742, s32[]{:T(128)} %get-tuple-element.741, bf16[1024,12576]{1,0:T(8,128)(2,1)} %get-tuple-element.752, f32[256]{0:T(256)S(1)} %bitcast.333, s32[256]{0:T(256)S(1)} %bitcast.332, f32[256]{0:T(256)S(1)} %bitcast.334, ...), kind=kOutput, calls=%fused_computation.22.clone.1.clone | convolution fusion | flops 13206208512 | bytes 53481472 | tf_op jit(solution)/shard_map/while/body/eval_jaxpr/lv,dv->ld/dot_general | solution.py:271
  760.6 33.9 %fusion.260 = f32[4,256,1024]{2,1,0:T(8,128)} fusion(f32[4,256,1024]{2,1,0:T(8,128)} %get-tuple-element.742, s32[]{:T(128)} %get-tuple-element.741, bf16[1024,12576]{1,0:T(8,128)(2,1)} %get-tuple-element.752, f32[256]{0:T(256)S(1)} %bitcast.333, s32[256]{0:T(256)S(1)} %bitcast.332, f32[256]{0:T(256)S(1)} %bitcast.334, ...), kind=kOutput, calls=%fused_computation.22.clone.1.clone | convolution fusion | flops 13206208512 | bytes 53481472 | tf_op jit(solution)/shard_map/while/body/eval_jaxpr/lv,dv->ld/dot_general | solution.py:271
  794.5 34.0 %fusion.260 = f32[4,256,1024]{2,1,0:T(8,128)} fusion(f32[4,256,1024]{2,1,0:T(8,128)} %get-tuple-element.742, s32[]{:T(128)} %get-tuple-element.741, bf16[1024,12576]{1,0:T(8,128)(2,1)} %get-tuple-element.752, f32[256]{0:T(256)S(1)} %bitcast.333, s32[256]{0:T(256)S(1)} %bitcast.332, f32[256]{0:T(256)S(1)} %bitcast.334, ...), kind=kOutput, calls=%fused_computation.22.clone.1.clone | convolution fusion | flops 13206208512 | bytes 53481472 | tf_op jit(solution)/shard_map/while/body/eval_jaxpr/lv,dv->ld/dot_general | solution.py:271
  828.5 33.9 %fusion.260 = f32[4,256,1024]{2,1,0:T(8,128)} fusion(f32[4,256,1024]{2,1,0:T(8,128)} %get-tuple-element.742, s32[]{:T(128)} %get-tuple-element.741, bf16[1024,12576]{1,0:T(8,128)(2,1)} %get-tuple-element.752, f32[256]{0:T(256)S(1)} %bitcast.333, s32[256]{0:T(256)S(1)} %bitcast.332, f32[256]{0:T(256)S(1)} %bitcast.334, ...), kind=kOutput, calls=%fused_computation.22.clone.1.clone | convolution fusion | flops 13206208512 | bytes 53481472 | tf_op jit(solution)/shard_map/while/body/eval_jaxpr/lv,dv->ld/dot_general | solution.py:271
  863.2 153.4 %all-reduce.7.cloned.1.call-done = f32[1024,1024]{1,0:T(8,128)} async-done(((f32[1024,1024]{1,0:T(8,128)}), f32[1024,1024]{1,0:T(8,128)}) %all-reduce.7.cloned.1.call-update) | async-done | bytes 4194320 | tf_op jit(solution)/shard_map/psum | solution.py:282
  1054.3 140.7 %reduce-scatter.2.cloned.1.call-done = f32[8,32,128]{2,1,0:T(8,128)} async-done(((f32[8,1024,128]{2,1,0:T(8,128)}), f32[8,32,128]{2,1,0:T(8,128)}) %reduce-scatter.2.cloned.1.call-update) | async-done | bytes 131088 | tf_op jit(solution)/shard_map/reduce_scatter | solution.py:333
  1196.5 17.0 %psum.29 = f32[]{:T(128)} all-reduce(f32[]{:T(128)} %get-tuple-element.415), channel_id=1, replica_groups=mesh['dp'=8,'mp'=4] {'dp'}, use_global_device_ids=true, to_apply=%region_19.20 | all-reduce | flops 1 | bytes 8 | tf_op jit(solution)/shard_map/psum | solution.py:336
  1213.5 45.0 %psum.31 = f32[]{:T(128)} all-reduce(f32[]{:T(128)} %multiply_reduce_fusion.4), channel_id=1, replica_groups=mesh['dp'=8,'mp'=4] {'dp','mp'}, use_global_device_ids=true, to_apply=%region_29.30 | all-reduce | flops 1 | bytes 8 | tf_op jit(solution)/shard_map/psum | solution.py:335
  (328 shorter events, 118.5 us)
Async XLA Ops:
  8.0 121.1 %copy-start = (bf16[1024,1024]{1,0:T(8,128)(2,1)S(1)}, bf16[1024,1024]{1,0:T(8,128)(2,1)}, u32[]{:S(2)}) copy-start(bf16[1024,1024]{1,0:T(8,128)(2,1)} %param.42) | copy-start | bytes 6291460
  8.0 112.2 %all-reduce.5.cloned.1.call-start = ((), (), s32[]{:S(2)}) async-start(), calls=%async_computation.1 | async-start | bytes 4194304 | tf_op jit(solution)/shard_map/psum | solution.py:185
  30.7 114.8 %all-gather.8.cloned.1.call-start = ((), (), s32[]{:S(2)}) async-start(), calls=%async_computation.2 | async-start | bytes 2162688 | tf_op jit(solution)/shard_map/all_gather | solution.py:171
  31.5 421.0 %all-gather.12.cloned.1.call-start = ((), (), s32[]{:S(2)}) async-start(), calls=%async_computation.6 | async-start | bytes 20971520 | tf_op jit(solution)/shard_map/all_gather | solution.py:241
  31.7 437.3 %copy-start.57 = (f32[1,1024]{1,0:T(1,128)}, f32[1,1024]{1,0:T(1,128)S(1)}, u32[]{:S(2)}) copy-start(f32[1,1024]{1,0:T(1,128)S(1)} %get-tuple-element.447) | copy-start | bytes 12292
  31.9 119.4 %copy-start.45 = (f32[1024,8]{0,1:T(8,128)}, f32[1024,8]{0,1:T(8,128)S(1)}, u32[]{:S(2)}) copy-start(f32[1024,8]{0,1:T(8,128)S(1)} %get-tuple-element.452) | copy-start | bytes 98308
  31.9 119.4 %copy-start.47 = (f32[1024,8]{0,1:T(8,128)}, f32[1024,8]{0,1:T(8,128)S(1)}, u32[]{:S(2)}) copy-start(f32[1024,8]{0,1:T(8,128)S(1)} %get-tuple-element.453) | copy-start | bytes 98308
  147.1 14.4 %copy-start.44 = (bf16[1,1024,128]{2,1,0:T(8,128)(2,1)}, bf16[1,1024,128]{2,1,0:T(8,128)(2,1)S(1)}, u32[]{:S(2)}) copy-start(bf16[1,1024,128]{2,1,0:T(8,128)(2,1)S(1)} %get-tuple-element.423) | copy-start | bytes 786436
  151.3 9.3 copy-start.14
  152.6 8.0 copy-start.8
  167.9 415.0 %all-gather.10.cloned.1.call-start = ((), (), s32[]{:S(2)}) async-start(), calls=%async_computation.3 | async-start | bytes 29196288 | tf_op jit(solution)/shard_map/all_gather | solution.py:172
  173.6 843.0 %all-reduce.7.cloned.1.call-start = ((), (), s32[]{:S(2)}) async-start(), calls=%async_computation.4 | async-start | bytes 8388608 | tf_op jit(solution)/shard_map/psum | solution.py:282
  452.5 10.8 copy-start.6
  862.4 154.1 %copy-start.7 = (bf16[1024,1024]{1,0:T(8,128)(2,1)S(1)}, bf16[1024,1024]{1,0:T(8,128)(2,1)}, u32[]{:S(2)}) copy-start(bf16[1024,1024]{1,0:T(8,128)(2,1)} %all-reduce.5.cloned.1.call-done) | copy-start | bytes 6291460
  862.4 154.1 %copy-start.56 = (f32[1024]{0:T(1024)S(1)}, f32[1024]{0:T(1024)}, u32[]{:S(2)}) copy-start(f32[1024]{0:T(1024)} %copy-done.55) | copy-start | bytes 12292
  862.4 154.1 %copy-start.58 = (f32[1,1024]{1,0:T(1,128)S(1)}, f32[1,1024]{1,0:T(1,128)}, u32[]{:S(2)}) copy-start(f32[1,1024]{1,0:T(1,128)} %copy-done.57) | copy-start | bytes 12292
  862.5 332.5 %reduce-scatter.2.cloned.1.call-start = ((), (), s32[]{:S(2)}) async-start(), calls=%async_computation.5 | async-start | bytes 4325376 | tf_op jit(solution)/shard_map/reduce_scatter | solution.py:333
  863.1 158.0 %copy-start.62 = (f32[1024]{0:T(1024)S(1)}, f32[1024]{0:T(1024)}, u32[]{:S(2)}) copy-start(f32[1024]{0:T(1024)} %copy-done.61) | copy-start | bytes 12292
  863.2 158.0 %copy-start.60 = (f32[1024]{0:T(1024)S(1)}, f32[1024]{0:T(1024)}, u32[]{:S(2)}) copy-start(f32[1024]{0:T(1024)} %copy-done.59) | copy-start | bytes 12292
  1052.7 206.5 %copy-start.23 = (f32[8,128,128]{2,1,0:T(8,128)S(1)}, f32[8,128,128]{2,1,0:T(8,128)}, u32[]{:S(2)}) copy-start(f32[8,128,128]{2,1,0:T(8,128)} %param.49) | copy-start | bytes 1572868
  1052.7 206.5 %copy-start.53 = (f32[8,32,128]{2,1,0:T(8,128)S(1)}, f32[8,32,128]{2,1,0:T(8,128)}, u32[]{:S(2)}) copy-start(f32[8,32,128]{2,1,0:T(8,128)} %param.48) | copy-start | bytes 393220
  1052.7 206.5 %copy-start.54 = (f32[8,32,128]{2,1,0:T(8,128)S(1)}, f32[8,32,128]{2,1,0:T(8,128)}, u32[]{:S(2)}) copy-start(f32[8,32,128]{2,1,0:T(8,128)} %param.47) | copy-start | bytes 393220
  1052.7 208.0 %copy-start.43 = (f32[8,32,128]{2,1,0:T(8,128)S(1)}, f32[8,32,128]{2,1,0:T(8,128)}, u32[]{:S(2)}) copy-start(f32[8,32,128]{2,1,0:T(8,128)} %param.46) | copy-start | bytes 393220
  1052.7 209.6 %copy-start.1 = (bf16[1024,1024]{1,0:T(8,128)(2,1)S(1)}, bf16[1024,1024]{1,0:T(8,128)(2,1)}, u32[]{:S(2)}) copy-start(bf16[1024,1024]{1,0:T(8,128)(2,1)} %param.42) | copy-start | bytes 6291460
  (62 other events, 169.1 us)
Sparse Core Ops, SparseCore 0:
  30.9 89.3 all-reduce.4
  168.0 284.4 all-gather.11
  454.3 128.5 all-gather.9
  862.6 153.8 all-reduce.6
Sparse Core Ops, SparseCore 1:
  34.7 98.1 all-gather.7
  1054.4 140.5 reduce-scatter.1
